TPU v7x, 256 devices: a whole 4x4x8 slice. The times are simulated.
256 devices in a mesh: dp: 4 (over x), expert: 64 (over y, z, core).
Axes of the slice: x: 4, y: 4, z: 8, core: 2. Of those that a mesh axis runs over, the one named last changes fastest.
Arguments:
- tokens: bfloat16 [4096, 3584], P(('dp', 'expert')), may hold values from -6 to 6
- out_grad: bfloat16 [4096, 3584], P(('dp', 'expert')), may hold values from -6 to 6
- route_ids: int32 [4096, 8], P(('dp', 'expert')), may hold values from 0 to 127, all different within a row; in each aligned block of 16 rows (0 to 15, 16 to 31, ...) at most 2 rows name the same one
- route_probs: float32 [4096, 8], P(('dp', 'expert')), may hold values from 0.02 to 0.5
- w_gate: bfloat16 [128, 3584, 1024], P('expert', None, 'dp'), may hold values from -0.09375 to 0.09375
- w_up: bfloat16 [128, 3584, 1024], P('expert', None, 'dp'), may hold values from -0.09375 to 0.09375
- w_down: bfloat16 [128, 1024, 3584], P('expert', 'dp'), may hold values from -0.1875 to 0.1875
Outputs:
- in_grad: bfloat16 [4096, 3584], P(('dp', 'expert'))
Inputs may be any that keep to these rules, and one draw needn't show every extreme that they name: `route_ids`: the 8 ids of a token differ. Among the tokens of one device (aligned blocks of 16 rows) no expert is named more than 2 times, and in every draw some expert is named exactly 2 times there.
All inputs are finite; a program needn't handle non-finite values.
Results may differ from a plain program's by a relative error of at most 0.015.
Values may be sent and summed in bfloat16 or wider, within the bound.
No kernel may reach another device: no remote copies, remote signals or barrier semaphores. Data moves between devices by JAX's collectives and lax.ppermute only.
A program may use at most 128 MiB of HBM per device.

v0:
```python
import jax
import jax.numpy as jnp
from jax import lax
from jax.sharding import PartitionSpec as P

TOPK = 8


def slot_matches(flat_ids, experts, capacity):
    onehot = (flat_ids[:, None] == jnp.arange(experts, dtype=jnp.int32)[None, :]).astype(jnp.int32)
    earlier = jnp.cumsum(onehot, axis=0) - onehot
    slot_rank = jnp.sum(earlier * onehot, axis=1)
    slot_of = flat_ids * capacity + slot_rank
    return slot_of[None, :] == jnp.arange(experts * capacity, dtype=jnp.int32)[:, None]


def select_matrix(matches, tok_count):
    return jnp.sum(matches.reshape(matches.shape[0], tok_count, TOPK).astype(jnp.float32), axis=2)


def build_tiles(token_rows, grad_rows, matches, flat_probs):
    select = select_matrix(matches, token_rows.shape[0]).astype(jnp.bfloat16)
    slot_scale = jnp.sum(jnp.where(matches, flat_probs[None, :], 0.0), axis=1)
    x_rows = jnp.dot(select, token_rows, preferred_element_type=jnp.float32).astype(jnp.bfloat16)
    g_rows = (
        jnp.dot(select, grad_rows, preferred_element_type=jnp.float32) * slot_scale[:, None]
    ).astype(jnp.bfloat16)
    return jnp.stack([x_rows, g_rows])


def expert_grads(tiles, w_gate, w_up, w_down):
    x_rows = tiles[:, 0]
    g_rows = tiles[:, 1]
    gate_pre = jnp.einsum("nsecd,edh->nsech", x_rows, w_gate, preferred_element_type=jnp.float32)
    up_pre = jnp.einsum("nsecd,edh->nsech", x_rows, w_up, preferred_element_type=jnp.float32)
    hidden_grad = jnp.einsum("nsecd,ehd->nsech", g_rows, w_down, preferred_element_type=jnp.float32)
    sigmoid_a = jax.nn.sigmoid(gate_pre)
    gate_grad = (hidden_grad * up_pre * sigmoid_a * (1.0 + gate_pre * (1.0 - sigmoid_a))).astype(
        jnp.bfloat16
    )
    up_grad = (hidden_grad * gate_pre * sigmoid_a).astype(jnp.bfloat16)
    partial_value = jnp.einsum(
        "nsech,edh->nsecd", gate_grad, w_gate, preferred_element_type=jnp.float32
    )
    partial_value = partial_value + jnp.einsum(
        "nsech,edh->nsecd", up_grad, w_up, preferred_element_type=jnp.float32
    )
    return partial_value.astype(jnp.bfloat16)


def on_device(tokens, out_grad, route_ids, route_probs, w_gate, w_up, w_down):
    columns = lax.axis_size("expert")
    local_experts = w_gate.shape[0]
    experts = local_experts * columns
    tok_count, width = tokens.shape
    capacity = max(2, 2 * tok_count * TOPK // experts)
    slots = experts * capacity
    tile_shape = (2, columns, local_experts, capacity, width)
    own_matches = slot_matches(route_ids.reshape(-1), experts, capacity)
    tiles = build_tiles(tokens, out_grad, own_matches, route_probs.reshape(-1)).reshape(
        (1,) + tile_shape
    )
    received = lax.all_to_all(tiles, "expert", split_axis=2, concat_axis=2, tiled=True)
    partials = expert_grads(
        lax.all_gather(received, "dp", axis=0, tiled=True), w_gate, w_up, w_down
    )
    summed = lax.psum_scatter(
        partials.astype(jnp.float32).astype(jnp.bfloat16), "dp", scatter_dimension=0, tiled=True
    ).astype(jnp.float32)
    returned = lax.all_to_all(
        summed.astype(jnp.bfloat16), "expert", split_axis=1, concat_axis=1, tiled=True
    ).astype(summed.dtype)
    own_select = select_matrix(own_matches, tok_count)
    result = jnp.dot(own_select.T, returned.reshape(slots, width), precision=lax.Precision.HIGHEST)
    return result.astype(jnp.bfloat16)


def solution(mesh):
    placed = (
        P(("dp", "expert"), None),
        P(("dp", "expert"), None),
        P(("dp", "expert"), None),
        P(("dp", "expert"), None),
        P("expert", None, "dp"),
        P("expert", None, "dp"),
        P("expert", "dp", None),
    )
    return jax.shard_map(
        on_device, mesh=mesh, in_specs=placed, out_specs=P(("dp", "expert"), None), check_vma=False
    )
```

profile of v0, /device:TPU:1, one launch (start us, length us, event | category | flops | bytes accessed | tf_op | source)
XLA Modules:
  0.0 523.0 jit_solution(11787229914710495954)
XLA Ops:
  6.5 0.0 copy-start
  6.5 0.0 copy-start.4
  6.5 0.0 all-gather.2.cloned.1.call-start
  6.5 0.8 copy.26
  7.3 0.1 eq.35
  7.4 0.1 fusion.33
  7.5 0.2 reduce_window_sum.11
  7.7 0.2 select_reduce_fusion.1
  7.9 0.1 reduce_sum.34
  8.0 0.1 convert_reduce_fusion
  8.1 0.8 copy.28
  8.9 0.1 broadcast_in_dim.18
  9.0 0.1 select_reduce_fusion
  9.1 0.0 copy-done
  9.1 1.9 fusion.4
  11.0 3.9 stack.10
  14.9 0.0 copy-done.4
  14.9 1.9 convolution_convert_fusion
  16.8 4.7 stack.9
  21.6 6.4 %pad_maximum_fusion = bf16[1,2,64,2,2,3584]{5,4,0,3,1,2:T(2,128)(2,1)S(1)} fusion(bf16[1,1,64,2,2,3584]{5,4,0,3,1,2:T(2,128)(2,1)S(1)} %bitcast.88, bf16[1,1,64,2,2,3584]{5,4,0,3,1,2:T(2,128)(2,1)} %bitcast.89), kind=kLoop, calls=%fused_computation.11 | loop fusion | flops 1835008 | bytes 7340032 | tf_op jit(solution)/shard_map/stack | solution.py:28
  28.0 97.7 %all_to_all.10 = bf16[1,2,64,2,2,3584]{5,4,0,3,1,2:T(2,128)(2,1)S(1)} all-to-all(bf16[1,2,64,2,2,3584]{5,4,0,3,1,2:T(2,128)(2,1)S(1)} %pad_maximum_fusion), channel_id=1, replica_groups=mesh['dp'=4,'expert'=64] {'expert'}, dimensions={2} | all-to-all | bytes 7340032 | tf_op jit(solution)/shard_map/all_to_all | solution.py:63
  125.7 2.9 copy.31
  128.5 0.0 all-gather.2.cloned.1.call-update
  128.6 0.2 all-reduce.3.cloned.1.call-start
  128.8 135.5 %all-gather.2.cloned.1.call-done = bf16[4,2,64,2,2,3584]{5,2,4,0,3,1:T(8,128)(2,1)} async-done(((bf16[1,2,64,2,2,3584]{5,2,4,0,3,1:T(8,128)(2,1)}), bf16[4,2,64,2,2,3584]{5,2,4,0,3,1:T(8,128)(2,1)}) %all-gather.2.cloned.1.call-update) | async-done | bytes 14680080 | tf_op jit(solution)/shard_map/all_gather | solution.py:65
  264.3 0.0 copy-start.5
  264.3 6.3 %fusion.14 = f32[4,64,2,2,256]{4,1,3,0,2:T(8,128)S(1)} fusion(bf16[2,3584,256]{2,1,0:T(8,128)(2,1)} %param.11, bf16[4,2,64,2,2,3584]{5,2,4,0,3,1:T(8,128)(2,1)} %all-gather.2.cloned.1.call-done), kind=kOutput, calls=%fused_computation.19 | convolution fusion | flops 1879048192 | bytes 12058624 | tf_op jit(solution)/shard_map/nsecd,edh->nsech/dot_general | solution.py:34
  270.7 2.0 copy-done.5
  272.6 0.0 copy-start.3
  272.6 4.3 fusion.17
  276.9 0.0 copy-done.3
  276.9 0.0 copy-start.2
  276.9 5.5 %fusion.29 = bf16[4,64,2,2,256]{4,1,3,0,2:T(8,128)(2,1)S(1)} fusion(f32[4,64,2,2,256]{4,1,3,0,2:T(8,128)S(1)} %fusion.17, bf16[2,3584,256]{2,1,0:T(8,128)(2,1)S(1)} %copy-done.3, bf16[4,2,64,2,2,3584]{5,2,4,0,3,1:T(8,128)(2,1)} %all-gather.2.cloned.1.call-done, f32[4,64,2,2,256]{4,1,3,0,2:T(8,128)S(1)} %fusion.14), kind=kOutput, calls=%fused_computation.24 | convolution fusion | flops 1881669632 | bytes 13631488 | tf_op jit(solution)/shard_map/nsecd,edh->nsech/dot_general | solution.py:35
  282.4 0.0 copy-done.2
  282.4 7.3 %fusion.5 = f32[2,4,64,2,3584]{4,2,3,1,0:T(8,128)} fusion(bf16[4,64,2,2,256]{4,1,3,0,2:T(8,128)(2,1)S(1)} %fusion.29, bf16[2,3584,256]{2,1,0:T(8,128)(2,1)S(1)} %copy-done.2), kind=kOutput, calls=%fused_computation.12 | convolution fusion | flops 1879048192 | bytes 18874368 | tf_op jit(solution)/shard_map/nsech,edh->nsecd/dot_general | solution.py:42
  289.8 11.3 %fusion.1 = bf16[4,64,2,2,3584]{4,1,3,0,2:T(8,128)(2,1)} fusion(f32[2,4,64,2,3584]{4,2,3,1,0:T(8,128)} %fusion.5, bf16[2,3584,256]{2,1,0:T(8,128)(2,1)} %param.12, f32[4,64,2,2,256]{4,1,3,0,2:T(8,128)S(1)} %fusion.17, f32[4,64,2,2,256]{4,1,3,0,2:T(8,128)S(1)} %fusion.14), kind=kOutput, calls=%fused_computation.4 | convolution fusion | flops 1887961088 | bytes 27787264 | tf_op jit(solution)/shard_map/nsech,edh->nsecd/dot_general | solution.py:45
  301.1 0.0 copy-start.6
  301.1 0.0 all-reduce.3.cloned.1.call-update
  301.1 0.6 copy-done.6
  301.8 0.6 dynamic-slice
  302.4 148.9 %all-reduce.3.cloned.1.call-done = bf16[4,64,2,2,3584]{4,1,3,0,2:T(8,128)(2,1)} async-done(((bf16[4,64,2,2,3584]{4,1,3,0,2:T(8,128)(2,1)}), bf16[4,64,2,2,3584]{4,1,3,0,2:T(8,128)(2,1)}) %all-reduce.3.cloned.1.call-update) | async-done | bytes 7340048
  451.3 2.3 constant_dynamic-slice_fusion
  453.6 1.9 copy.32
  455.5 0.0 copy-start.1
  455.5 56.1 %all_to_all.11 = bf16[1,64,2,2,3584]{4,3,0,2,1:T(2,128)(2,1)S(1)} all-to-all(bf16[1,64,2,2,3584]{4,3,0,2,1:T(2,128)(2,1)S(1)} %copy.32), channel_id=1, replica_groups=mesh['dp'=4,'expert'=64] {'expert'}, dimensions={1} | all-to-all | bytes 3670016 | tf_op jit(solution)/shard_map/all_to_all | solution.py:70
  511.6 1.7 reshape.31
  513.2 3.0 convolution_convert_fusion.1
  516.2 0.0 copy-done.1
  (2 shorter events, 0.0 us)
Async XLA Ops:
  6.5 2.5 copy-start
  6.5 8.4 %copy-start.4 = (bf16[16,3584]{1,0:T(8,128)(2,1)S(1)}, bf16[16,3584]{1,0:T(8,128)(2,1)}, u32[]{:S(2)}) copy-start(bf16[16,3584]{1,0:T(8,128)(2,1)} %param.7) | copy-start | bytes 344068
  6.5 257.8 %all-gather.2.cloned.1.call-start = ((), (), s32[]{:S(2)}) async-start(), calls=%async_computation.2 | async-start | bytes 18350080 | tf_op jit(solution)/shard_map/all_gather | solution.py:65
  128.6 322.8 %all-reduce.3.cloned.1.call-start = ((), (), s32[]{:S(2)}) async-start(), calls=%async_computation.3 | async-start | bytes 14680064
  264.3 8.3 %copy-start.5 = (bf16[4,2,64,2,2,3584]{5,2,4,0,3,1:T(8,128)(2,1)S(1)}, bf16[4,2,64,2,2,3584]{5,2,4,0,3,1:T(8,128)(2,1)}, u32[]{:S(2)}) copy-start(bf16[4,2,64,2,2,3584]{5,2,4,0,3,1:T(8,128)(2,1)} %all-gather.2.cloned.1.call-done) | copy-start | bytes 44040196
  272.6 4.3 copy-start.3
  276.9 5.5 %copy-start.2 = (bf16[2,3584,256]{2,1,0:T(8,128)(2,1)S(1)}, bf16[2,3584,256]{2,1,0:T(8,128)(2,1)}, u32[]{:S(2)}) copy-start(bf16[2,3584,256]{2,1,0:T(8,128)(2,1)} %param.11) | copy-start | bytes 11010052
  301.1 0.7 copy-start.6
  455.5 60.7 %copy-start.1 = (bf16[16,3584]{1,0:T(8,128)(2,1)S(1)}, bf16[16,3584]{1,0:T(8,128)(2,1)}, u32[]{:S(2)}) copy-start(bf16[16,3584]{1,0:T(8,128)(2,1)} %param.8) | copy-start | bytes 344068
Sparse Core Ops, SparseCore 0:
  128.7 135.6 all-gather.1
  301.2 150.0 all-reduce.2
where the time goes:
time: 523 us
  waiting for transfers between devices  285 us (54%)
  blocking collectives  154 us (29%)
  matrix products  41.6 us (8%)
  local copies, waits for them, and re-layouts  22.3 us (4%)
  between operations  13.5 us (3%)
  other arithmetic  7.1 us (1%)
    unnamed x3, waiting for transfers between devices  149 us
    all_gather x1, waiting for transfers between devices, on_device(): lax.all_gather(received, 'dp', axis=0, tiled=True)  136 us
    all_to_all x1, blocking collectives, on_device(): lax.all_to_all(tiles, 'expert', split_axis=2, concat_axis=2, tiled=True)  97.7 us
    all_to_all x1, blocking collectives, on_device(): lax.all_to_all(summed.astype(jnp.bfloat16), 'expert', split_axis=1, conca...  56.1 us
    dot_general x1, matrix products, expert_grads(): jnp.einsum('nsech,edh->nsecd', up_grad, w_up, preferred_element_type=jnp....  11.3 us
  transfers between devices with their start and end apart: 2, of which 2 were waited for; matrix products, arithmetic and copies ran while one was open for 0% of the time, Pallas kernels for 0%

commit v1 on v0

--- a/solution.py
+++ b/solution.py
@@ -62,7 +62,12 @@
     )
     received = lax.all_to_all(tiles, "expert", split_axis=2, concat_axis=2, tiled=True)
     partials = expert_grads(
-        lax.all_gather(received, "dp", axis=0, tiled=True), w_gate, w_up, w_down
+        jnp.concatenate(
+            lax.all_to_all(jnp.stack([received] * lax.axis_size("dp")), "dp", 0, 0), axis=0
+        ),
+        w_gate,
+        w_up,
+        w_down,
     )
     summed = lax.psum_scatter(
         partials.astype(jnp.float32).astype(jnp.bfloat16), "dp", scatter_dimension=0, tiled=True

time: 523 us -> 544 us (1.040)
  blocking collectives: 154 us -> 318 us
  waiting for transfers between devices: 285 us -> 144 us
    all_to_all x0 -> x1, blocking collectives: none -> 165 us  [on_device(): lax.all_to_all(jnp.stack([received] * lax.axis_size('dp')), 'dp', 0, 0)]
    all_gather x1 -> x0, waiting for transfers between devices: 136 us -> none  [on_device(): lax.all_gather(received, 'dp', axis=0, tiled=True)]
    unnamed x3 -> x2, waiting for transfers between devices: 149 us -> 144 us
  transfers between devices with their start and end apart: 2 -> 1, of which waited for: 2 -> 1; matrix products, arithmetic and copies ran while one was open for 0% -> 0% of each run, Pallas kernels for 0% -> 0%
where the time goes in v1:
time: 544 us; the launch traced here: 543 us
  blocking collectives  318 us (58%)
  waiting for transfers between devices  144 us (26%)
  matrix products  37.6 us (7%)
  local copies, waits for them, and re-layouts  22.9 us (4%)
  between operations  13.5 us (2%)
  other arithmetic  7.1 us (1%)
    all_to_all x1, blocking collectives, on_device(): lax.all_to_all(jnp.stack([received] * lax.axis_size('dp')), 'dp', 0, 0)  165 us
    unnamed x2, waiting for transfers between devices  144 us
    all_to_all x1, blocking collectives, on_device(): lax.all_to_all(tiles, 'expert', split_axis=2, concat_axis=2, tiled=True)  97.7 us
    all_to_all x1, blocking collectives, on_device(): lax.all_to_all(summed.astype(jnp.bfloat16), 'expert', split_axis=1, conca...  56.1 us
    dot_general x1, matrix products, expert_grads(): jnp.einsum('nsech,edh->nsecd', up_grad, w_up, preferred_element_type=jnp....  11.4 us
  transfers between devices with their start and end apart: 1, of which 1 were waited for; matrix products, arithmetic and copies ran while one was open for 0% of the time, Pallas kernels for 0%

profile of v1, /device:TPU:1, one launch (start us, length us, event | category | flops | bytes accessed | tf_op | source)
XLA Modules:
  0.0 543.2 jit_solution(14633718708053179238)
XLA Ops:
  6.5 0.0 copy-start
  6.5 0.0 copy-start.6
  6.5 0.0 all-reduce.3.cloned.1.call-start
  6.5 0.8 copy.25
  7.3 0.1 eq.35
  7.4 0.1 fusion.33
  7.5 0.2 reduce_window_sum.11
  7.7 0.2 select_reduce_fusion.1
  7.9 0.1 reduce_sum.34
  8.0 0.1 convert_reduce_fusion
  8.1 0.8 copy.27
  8.9 0.1 broadcast_in_dim.18
  9.0 0.1 select_reduce_fusion
  9.1 0.0 copy-done
  9.1 1.9 fusion.4
  11.0 3.9 stack.17
  14.9 0.0 copy-done.6
  14.9 1.9 convolution_convert_fusion
  16.8 4.7 stack.16
  21.6 6.4 %pad_maximum_fusion = bf16[1,2,64,2,2,3584]{5,4,3,1,0,2:T(2,128)(2,1)S(1)} fusion(bf16[1,1,64,2,2,3584]{5,4,3,1,0,2:T(2,128)(2,1)S(1)} %bitcast.96, bf16[1,1,64,2,2,3584]{5,4,3,1,0,2:T(2,128)(2,1)} %bitcast.97), kind=kLoop, calls=%fused_computation.12 | loop fusion | flops 1835008 | bytes 7340032 | tf_op jit(solution)/shard_map/stack | solution.py:28
  28.0 97.7 %all_to_all.18 = bf16[1,2,64,2,2,3584]{5,4,3,1,0,2:T(2,128)(2,1)S(1)} all-to-all(bf16[1,2,64,2,2,3584]{5,4,3,1,0,2:T(2,128)(2,1)S(1)} %pad_maximum_fusion), channel_id=1, replica_groups=mesh['dp'=4,'expert'=64] {'expert'}, dimensions={2} | all-to-all | bytes 7340032 | tf_op jit(solution)/shard_map/all_to_all | solution.py:63
  125.7 1.1 copy.30
  126.7 1.8 stack.19
  128.5 164.6 %all_to_all.19 = bf16[4,1,2,64,2,2,3584]{6,3,5,4,2,1,0:T(8,128)(2,1)S(1)} all-to-all(bf16[4,1,2,64,2,2,3584]{6,3,5,4,2,1,0:T(8,128)(2,1)S(1)} %stack.19), channel_id=1, replica_groups=mesh['dp'=4,'expert'=64] {'dp'}, dimensions={0} | all-to-all | bytes 29360128 | tf_op jit(solution)/shard_map/all_to_all | solution.py:66
  293.1 0.0 copy-start.2
  293.2 2.6 copy.39
  295.7 0.0 copy-done.2
  295.8 3.1 fusion.14
  298.8 5.3 fusion.17
  304.1 0.0 copy-done.3
  304.1 3.8 fusion.29
  307.9 0.0 copy-start.4
  307.9 0.0 copy-start.5
  307.9 7.3 %fusion.5 = f32[2,4,64,2,3584]{4,2,3,1,0:T(8,128)} fusion(bf16[4,64,2,2,256]{4,1,3,0,2:T(8,128)(2,1)S(1)} %fusion.29, bf16[2,3584,256]{2,1,0:T(8,128)(2,1)S(1)} %copy-done.2), kind=kOutput, calls=%fused_computation.13 | convolution fusion | flops 1879048192 | bytes 18874368 | tf_op jit(solution)/shard_map/nsech,edh->nsecd/dot_general | solution.py:42
  315.2 0.0 copy-done.4
  315.2 0.0 copy-done.5
  315.2 11.4 %fusion.1 = bf16[4,64,2,2,3584]{4,1,3,0,2:T(8,128)(2,1)} fusion(f32[2,4,64,2,3584]{4,2,3,1,0:T(8,128)} %fusion.5, bf16[2,3584,256]{2,1,0:T(8,128)(2,1)} %param.12, f32[4,64,2,2,256]{4,1,3,0,2:T(8,128)S(1)} %copy-done.5, f32[4,64,2,2,256]{4,1,3,0,2:T(8,128)S(1)} %copy-done.4), kind=kOutput, calls=%fused_computation.5 | convolution fusion | flops 1887961088 | bytes 27787264 | tf_op jit(solution)/shard_map/nsech,edh->nsecd/dot_general | solution.py:45
  326.6 0.0 all-reduce.3.cloned.1.call-update
  326.6 0.6 copy-done.7
  327.3 0.6 dynamic-slice
  327.8 143.6 %all-reduce.3.cloned.1.call-done = bf16[4,64,2,2,3584]{4,1,3,0,2:T(8,128)(2,1)} async-done(((bf16[4,64,2,2,3584]{4,1,3,0,2:T(8,128)(2,1)}), bf16[4,64,2,2,3584]{4,1,3,0,2:T(8,128)(2,1)}) %all-reduce.3.cloned.1.call-update) | async-done | bytes 7340048
  471.5 2.3 constant_dynamic-slice_fusion
  473.7 1.9 copy.32
  475.6 0.0 copy-start.1
  475.6 56.1 %all_to_all.20 = bf16[1,64,2,2,3584]{4,3,0,2,1:T(2,128)(2,1)S(1)} all-to-all(bf16[1,64,2,2,3584]{4,3,0,2,1:T(2,128)(2,1)S(1)} %copy.32), channel_id=1, replica_groups=mesh['dp'=4,'expert'=64] {'expert'}, dimensions={1} | all-to-all | bytes 3670016 | tf_op jit(solution)/shard_map/all_to_all | solution.py:75
  531.7 1.7 reshape.38
  533.4 3.0 convolution_convert_fusion.1
  536.3 0.0 copy-done.1
  (4 shorter events, 0.0 us)
Async XLA Ops:
  6.5 2.5 copy-start
  6.5 8.4 %copy-start.6 = (bf16[16,3584]{1,0:T(8,128)(2,1)S(1)}, bf16[16,3584]{1,0:T(8,128)(2,1)}, u32[]{:S(2)}) copy-start(bf16[16,3584]{1,0:T(8,128)(2,1)} %param.7) | copy-start | bytes 344068
  6.5 464.9 %all-reduce.3.cloned.1.call-start = ((), (), s32[]{:S(2)}) async-start(), calls=%async_computation.3 | async-start | bytes 14680064
  293.1 2.6 copy-start.2
  298.8 5.3 copy-start.3
  307.9 7.4 %copy-start.4 = (f32[4,64,2,2,256]{4,1,3,0,2:T(8,128)S(1)}, f32[4,64,2,2,256]{4,1,3,0,2:T(8,128)}, u32[]{:S(2)}) copy-start(f32[4,64,2,2,256]{4,1,3,0,2:T(8,128)} %fusion.14) | copy-start | bytes 3145732
  307.9 7.3 %copy-start.5 = (f32[4,64,2,2,256]{4,1,3,0,2:T(8,128)S(1)}, f32[4,64,2,2,256]{4,1,3,0,2:T(8,128)}, u32[]{:S(2)}) copy-start(f32[4,64,2,2,256]{4,1,3,0,2:T(8,128)} %fusion.17) | copy-start | bytes 3145732
  326.6 0.7 copy-start.7
  475.6 60.7 %copy-start.1 = (bf16[16,3584]{1,0:T(8,128)(2,1)S(1)}, bf16[16,3584]{1,0:T(8,128)(2,1)}, u32[]{:S(2)}) copy-start(bf16[16,3584]{1,0:T(8,128)(2,1)} %param.8) | copy-start | bytes 344068
Sparse Core Ops, SparseCore 0:
  326.7 144.6 all-reduce.2
